TPU v7x, 32 devices: a whole 2x2x4 slice. The times are simulated.
32 devices in a mesh: wa: 16 (over z, y, core), gy: 2 (over x).
Axes of the slice: x: 2, y: 2, z: 4, core: 2. Of those that a mesh axis runs over, the one named last changes fastest.
Arguments:
- input_moments: float32 [120, 128, 32], P(None, 'wa', 'gy'), may hold values from -6 to 6
- solid_cell_mask: int32 [128, 32], P('wa', 'gy'), may hold values 0 or 1
- collision_coefficients: float32 [120, 120], replicated, may hold values from -0.5 to 0.5
- relaxation_rates: float32 [120], replicated, may hold values from 0.1 to 1
Outputs:
- final_state: float32 [120, 128, 32], P(None, 'wa', 'gy')
All inputs are finite; a program needn't handle non-finite values. No bound on the sum of `solid_cell_mask` on one device may be relied on, other than what follows from the above.
Results may differ from a plain program's by a relative error of at most 0.0003.
Values sent between devices are 32-bit elements; how exact they have to be, the bound alone decides.
No kernel may reach another device: no remote copies, remote signals or barrier semaphores. Data moves between devices by JAX's collectives and lax.ppermute only.
A program may use at most 64 MiB of HBM per device.

v0:
```python
import math
import jax
import jax.numpy as jnp
import numpy as np
from jax import lax
from jax.sharding import PartitionSpec as P

DEG = 7
ITERS = 2
highest_degree = lax.Precision.HIGHEST
axial_step = 0.2
cross_step = 0.2
collide_step = 0.5


def shifted(value, axis, by):
    count = lax.axis_size(axis)
    return lax.ppermute(value, axis, [(i, (i + by) % count) for i in range(count)])


def from_behind(value, axis, by):
    count = lax.axis_size(axis)
    pairs = [(i, i + by) for i in range(count) if 0 <= i + by < count]
    return lax.ppermute(value, axis, pairs)


def moment_table():
    entries = []
    for degree_now in range(DEG + 1):
        for first_k in range(degree_now, -1, -1):
            for second_k in range(degree_now - first_k, -1, -1):
                entries.append((first_k, second_k, degree_now - first_k - second_k))
    return entries


def hermite_value(order, point):
    previous = 1.0
    current_moments = point
    for level in range(1, order):
        previous, current_moments = (current_moments, point * current_moments - level * previous)
    return current_moments


def largest_root(order):
    upper = 2.0 * math.sqrt(order) + 1.0
    value_high = hermite_value(order, upper)
    lower = upper
    for trial in range(100000):
        lower = lower - 0.001
        value_low = hermite_value(order, lower)
        if (value_low > 0.0) != (value_high > 0.0):
            break
        upper = lower
        value_high = value_low
    for repeat in range(80):
        middle = 0.5 * (lower + upper)
        value_mid = hermite_value(order, middle)
        if (value_mid > 0.0) == (value_high > 0.0):
            upper = middle
            value_high = value_mid
        else:
            lower = middle
    return 0.5 * (lower + upper)


def coupling(entries, lookup, direction):
    matrix = np.zeros((len(entries), len(entries)), dtype=np.float32)
    for position, moment in enumerate(entries):
        raised = list(moment)
        raised[direction] += 1
        raised = tuple(raised)
        if raised in lookup:
            partner = lookup[raised]
            matrix[position, partner] = math.sqrt(moment[direction] + 1)
            matrix[partner, position] = math.sqrt(moment[direction] + 1)
    return matrix


def to_float(table):
    return jnp.asarray(table, dtype=jnp.float32)


def operator_tables():
    entries = moment_table()
    number = len(entries)
    lookup = {moment: position for position, moment in enumerate(entries)}
    axial_matrix = coupling(entries, lookup, 0)
    cross_matrix = coupling(entries, lookup, 1)
    degrees = np.array([sum(moment) for moment in entries])
    degree_band_mask = (
        (np.abs(degrees[:, None] - degrees[None, :]) <= 1)
        & (degrees[:, None] >= 2)
        & (degrees[None, :] >= 2)
    ).astype(np.float32)
    unit_rows = [lookup[1, 0, 0], lookup[0, 1, 0], lookup[0, 0, 1]]
    first_selection = np.zeros((number, number), dtype=np.float32)
    second_selection = np.zeros((number, number), dtype=np.float32)
    moment_weights = np.zeros(number, dtype=np.float32)
    for position, moment in enumerate(entries):
        if sum(moment) == 2:
            raised = [direction for direction in range(3) for repeat in range(moment[direction])]
            first_selection[position, unit_rows[raised[0]]] = 1.0
            second_selection[position, unit_rows[raised[1]]] = 1.0
            moment_weights[position] = 1.0 / math.sqrt(2.0) if raised[0] == raised[1] else 1.0
    relaxed = (degrees >= 2).astype(np.float32)
    density = (degrees == 0).astype(np.float32)
    speed_bound = largest_root(DEG + 1)
    return (
        to_float(axial_matrix),
        to_float(cross_matrix),
        to_float(degree_band_mask),
        to_float(first_selection),
        to_float(second_selection),
        to_float(moment_weights),
        to_float(relaxed),
        to_float(density),
        speed_bound,
    )


def wave_numbers(length):
    position = jnp.arange(length, dtype=jnp.int32)
    signed = jnp.where(position < length // 2, position, position - length)
    return signed.astype(jnp.float32) * (axial_step * 2.0 * math.pi / length)


def fourier_tables(length):
    position = jnp.arange(length, dtype=jnp.int32)
    phase_index = position[:, None] * position[None, :] % length
    angles = phase_index.astype(jnp.float32) * (2.0 * math.pi / length)
    return (jnp.cos(angles), jnp.sin(angles))


def phase_series(real_part, imag_part, axial_matrix, wave_scale):
    total_real, total_imag = (real_part, imag_part)
    term_real, term_imag = (real_part, imag_part)
    for term_order in range(1, 5):
        pushed_real = (
            jnp.einsum("js,suv->juv", axial_matrix, term_real, precision=highest_degree)
            * wave_scale[None, :, None]
        )
        pushed_imag = (
            jnp.einsum("js,suv->juv", axial_matrix, term_imag, precision=highest_degree)
            * wave_scale[None, :, None]
        )
        term_real, term_imag = (pushed_imag / term_order, -pushed_real / term_order)
        total_real = total_real + term_real
        total_imag = total_imag + term_imag
    return (total_real, total_imag)


def axial_update(line_field, cosine_table, sine_table, axial_matrix, wave_scale):
    length = line_field.shape[1]
    real_part = jnp.einsum("mxl,xk->mkl", line_field, cosine_table, precision=highest_degree)
    imag_part = -jnp.einsum("mxl,xk->mkl", line_field, sine_table, precision=highest_degree)
    total_real, total_imag = phase_series(real_part, imag_part, axial_matrix, wave_scale)
    restored = jnp.einsum("mkl,kx->mxl", total_real, cosine_table, precision=highest_degree)
    restored = restored - jnp.einsum(
        "mkl,kx->mxl", total_imag, sine_table, precision=highest_degree
    )
    return restored / length


def cross_update(current_moments, lower_rim, upper_rim, cross_matrix, speed_bound):
    central = jnp.einsum(
        "js,suv->juv", cross_matrix, upper_rim - lower_rim, precision=highest_degree
    )
    return current_moments - cross_step * (
        0.5 * central - 0.5 * speed_bound * (upper_rim - 2.0 * current_moments + lower_rim)
    )


def apply_walls(current_moments, mask_float, density):
    return current_moments * (1.0 - mask_float[None, :, :] * (1.0 - density)[:, None, None])


def apply_collisions(
    current_moments,
    collision_band,
    first_selection,
    second_selection,
    moment_weights,
    relaxation_applied,
):
    first_part = jnp.einsum(
        "js,suv->juv", first_selection, current_moments, precision=highest_degree
    )
    second_part = jnp.einsum(
        "js,suv->juv", second_selection, current_moments, precision=highest_degree
    )
    target = moment_weights[:, None, None] * first_part * second_part
    moment_mixing = jnp.einsum(
        "js,suv->juv", collision_band, current_moments, precision=highest_degree
    )
    return current_moments + collide_step * (
        moment_mixing - relaxation_applied[:, None, None] * (current_moments - target)
    )


def local(input_moments, solid_cell_mask, collision_coefficients, relaxation_rates):
    (
        axial_matrix,
        cross_matrix,
        degree_band_mask,
        first_selection,
        second_selection,
        moment_weights,
        relaxed,
        density,
        speed_bound,
    ) = operator_tables()
    collision_band = collision_coefficients * degree_band_mask
    relaxation_applied = relaxation_rates * relaxed
    length = input_moments.shape[1] * lax.axis_size("wa")
    cosine_table, sine_table = fourier_tables(length)
    wave_scale = wave_numbers(length)
    line_field = lax.all_to_all(input_moments, "wa", split_axis=2, concat_axis=1, tiled=True)
    mask_float = lax.all_to_all(
        solid_cell_mask, "wa", split_axis=1, concat_axis=0, tiled=True
    ).astype(jnp.float32)
    position_wa = lax.axis_index("wa")
    last_wa = lax.axis_size("wa") - 1
    for step_index in range(ITERS):
        line_field = axial_update(line_field, cosine_table, sine_table, axial_matrix, wave_scale)
        from_lower = shifted(line_field[:, :, -1:], "wa", 1)
        across_lower = from_behind(from_lower, "gy", 1)
        lower_line = jnp.where(position_wa == 0, across_lower, from_lower)
        from_upper = shifted(line_field[:, :, :1], "wa", -1)
        across_upper = from_behind(from_upper, "gy", -1)
        upper_line = jnp.where(position_wa == last_wa, across_upper, from_upper)
        padded = jnp.concatenate([lower_line, line_field, upper_line], axis=2)
        line_field = cross_update(
            line_field, padded[:, :, :-2], padded[:, :, 2:], cross_matrix, speed_bound
        )
        line_field = apply_walls(line_field, mask_float, density)
        line_field = apply_collisions(
            line_field,
            collision_band,
            first_selection,
            second_selection,
            moment_weights,
            relaxation_applied,
        )
    return lax.all_to_all(line_field, "wa", split_axis=1, concat_axis=2, tiled=True)


def solution(mesh):
    in_specs = (P(None, "wa", "gy"), P("wa", "gy"), P(), P())
    out_specs = P(None, "wa", "gy")
    return jax.shard_map(local, mesh=mesh, in_specs=in_specs, out_specs=out_specs, check_vma=False)
```

profile of v0, /device:TPU:0, one launch (start us, length us, event | category | flops | bytes accessed | tf_op | source)
XLA Modules:
  0.0 70.9 jit_solution(14473174839798971628)
XLA Ops:
  0.0 1.5 %copy.19 = f32[120,8,16]{0,1,2:T(8,128)} copy(f32[120,8,16]{0,2,1:T(8,128)} %param.12) | data formatting | bytes 122880 | tf_op args[0]
  1.5 7.4 %all-to-all-start = ((f32[120,8,16]{0,1,2:T(8,128)}), f32[120,8,16]{0,1,2:T(8,128)S(1)}, u32[]{:S(2)}, u32[]{:S(2)}) async-start(f32[120,8,16]{0,1,2:T(8,128)} %copy.19), calls=%async_computation | async-start | bytes 131072 | tf_op jit(solution)/shard_map/all_to_all | solution.py:217
  8.9 6.9 %all-to-all-done = f32[120,8,16]{0,1,2:T(8,128)S(1)} async-done(((f32[120,8,16]{0,1,2:T(8,128)}), f32[120,8,16]{0,1,2:T(8,128)S(1)}, u32[]{:S(2)}, u32[]{:S(2)}) %all-to-all-start) | async-done | bytes 61472 | tf_op jit(solution)/shard_map/all_to_all | solution.py:217
  15.8 0.5 fusion.59
  17.1 0.5 convolution_negate_fusion.1
  18.4 0.3 fusion.38
  18.9 0.5 fusion.92
  19.5 0.5 convolution_subtract_fusion.1
  20.1 4.4 %collective-permute-start = (f32[120,128,1]{1,0,2:T(8,128)S(1)}, f32[120,128,1]{1,0,2:T(8,128)S(1)}, u32[]{:S(2)}, u32[]{:S(2)}) collective-permute-start(f32[120,128,1]{1,0,2:T(8,128)S(1)} %multiply_bitcast_fusion.1), channel_id=1, source_target_pairs={{0,30},{2,0},{4,2},{6,4},{8,6},{10,8},{12,10},{14,12},{16,14},{18,... | collective-permute-start | bytes 184328 | tf_op jit(solution)/shard_map/ppermute | solution.py:18
  24.5 0.7 copy.20
  25.2 3.5 %all-to-all-start.1 = ((s32[8,16,1]{0,2,1:T(1,128)}), s32[8,16,1]{0,2,1:T(1,128)S(1)}, u32[]{:S(2)}, u32[]{:S(2)}) async-start(s32[8,16,1]{0,2,1:T(1,128)} %copy.20), calls=%async_computation.1 | async-start | bytes 16384 | tf_op jit(solution)/shard_map/all_to_all | solution.py:218
  28.7 0.6 copy-done.9
  29.4 3.4 %collective-permute-start.3 = (f32[120,128,1]{1,0,2:T(8,128)S(1)}, f32[120,128,1]{1,0,2:T(8,128)S(1)}, u32[]{:S(2)}, u32[]{:S(2)}) collective-permute-start(f32[120,128,1]{1,0,2:T(8,128)S(1)} %collective-permute-done.2), channel_id=1, source_target_pairs={{0,1},{2,3},{4,5},{6,7},{8,9},{10,11},{12,13},{14,15},{16,17},{18,... | collective-permute-start | bytes 184328 | tf_op jit(solution)/shard_map/ppermute | solution.py:24
  32.8 1.3 %collective-permute-start.1 = (f32[120,128,1]{1,0,2:T(8,128)S(1)}, f32[120,128,1]{1,0,2:T(8,128)S(1)}, u32[]{:S(2)}, u32[]{:S(2)}) collective-permute-start(f32[120,128,1]{1,0,2:T(8,128)S(1)} %collective-permute-done), channel_id=1, source_target_pairs={{1,0},{3,2},{5,4},{7,6},{9,8},{11,10},{13,12},{15,14},{17,16},{19,... | collective-permute-start | bytes 184328 | tf_op jit(solution)/shard_map/ppermute | solution.py:24
  34.1 0.9 %all-to-all-done.1 = s32[8,16,1]{0,2,1:T(1,128)S(1)} async-done(((s32[8,16,1]{0,2,1:T(1,128)}), s32[8,16,1]{0,2,1:T(1,128)S(1)}, u32[]{:S(2)}, u32[]{:S(2)}) %all-to-all-start.1) | async-done | bytes 544 | tf_op jit(solution)/shard_map/all_to_all | solution.py:218
  35.2 3.8 %collective-permute-done.1 = f32[120,128,1]{1,0,2:T(8,128)S(1)} collective-permute-done((f32[120,128,1]{1,0,2:T(8,128)S(1)}, f32[120,128,1]{1,0,2:T(8,128)S(1)}, u32[]{:S(2)}, u32[]{:S(2)}) %collective-permute-start.1) | collective-permute-done | bytes 61472 | tf_op jit(solution)/shard_map/ppermute | solution.py:24
  39.0 0.3 fusion.42
  39.5 0.6 copy-done.3
  40.6 0.5 convolution_negate_fusion
  41.1 0.5 fusion.90
  43.2 0.3 fusion.48
  43.7 0.5 fusion.88
  44.2 0.5 convolution_subtract_fusion
  44.8 4.4 %collective-permute-start.4 = (f32[120,128,1]{1,0,2:T(8,128)S(1)}, f32[120,128,1]{1,0,2:T(8,128)S(1)}, u32[]{:S(2)}, u32[]{:S(2)}) collective-permute-start(f32[120,128,1]{1,0,2:T(8,128)S(1)} %multiply_bitcast_fusion), channel_id=1, source_target_pairs={{0,30},{2,0},{4,2},{6,4},{8,6},{10,8},{12,10},{14,12},{16,14},{18,... | collective-permute-start | bytes 184328 | tf_op jit(solution)/shard_map/ppermute | solution.py:18
  49.3 2.0 %collective-permute-done.6 = f32[120,128,1]{1,0,2:T(8,128)S(1)} collective-permute-done((f32[120,128,1]{1,0,2:T(8,128)S(1)}, f32[120,128,1]{1,0,2:T(8,128)S(1)}, u32[]{:S(2)}, u32[]{:S(2)}) %collective-permute-start.6) | collective-permute-done | bytes 61472 | tf_op jit(solution)/shard_map/ppermute | solution.py:18
  51.2 1.6 %collective-permute-start.7 = (f32[120,128,1]{1,0,2:T(8,128)S(1)}, f32[120,128,1]{1,0,2:T(8,128)S(1)}, u32[]{:S(2)}, u32[]{:S(2)}) collective-permute-start(f32[120,128,1]{1,0,2:T(8,128)S(1)} %collective-permute-done.6), channel_id=1, source_target_pairs={{0,1},{2,3},{4,5},{6,7},{8,9},{10,11},{12,13},{14,15},{16,17},{18,... | collective-permute-start | bytes 184328 | tf_op jit(solution)/shard_map/ppermute | solution.py:24
  52.8 1.3 %collective-permute-start.5 = (f32[120,128,1]{1,0,2:T(8,128)S(1)}, f32[120,128,1]{1,0,2:T(8,128)S(1)}, u32[]{:S(2)}, u32[]{:S(2)}) collective-permute-start(f32[120,128,1]{1,0,2:T(8,128)S(1)} %collective-permute-done.4), channel_id=1, source_target_pairs={{1,0},{3,2},{5,4},{7,6},{9,8},{11,10},{13,12},{15,14},{17,16},{19,... | collective-permute-start | bytes 184328 | tf_op jit(solution)/shard_map/ppermute | solution.py:24
  54.1 0.5 collective-permute-done.7
  54.7 4.3 %collective-permute-done.5 = f32[120,128,1]{1,0,2:T(8,128)S(1)} collective-permute-done((f32[120,128,1]{1,0,2:T(8,128)S(1)}, f32[120,128,1]{1,0,2:T(8,128)S(1)}, u32[]{:S(2)}, u32[]{:S(2)}) %collective-permute-start.5) | collective-permute-done | bytes 61472 | tf_op jit(solution)/shard_map/ppermute | solution.py:24
  58.9 0.3 fusion.52
  60.1 10.2 %all_to_all.46 = f32[120,128,1]{0,2,1:T(1,128)S(1)} all-to-all(f32[120,128,1]{0,2,1:T(1,128)S(1)} %copy.21), channel_id=1, replica_groups=mesh['wa'=16,'gy'=2] {'wa'}, dimensions={1} | all-to-all | bytes 122880 | tf_op jit(solution)/shard_map/all_to_all | solution.py:244
  70.3 0.6 copy.22
  (54 shorter events, 5.5 us)
Async XLA Ops:
  1.5 14.3 %all-to-all-start = ((f32[120,8,16]{0,1,2:T(8,128)}), f32[120,8,16]{0,1,2:T(8,128)S(1)}, u32[]{:S(2)}, u32[]{:S(2)}) async-start(f32[120,8,16]{0,1,2:T(8,128)} %copy.19), calls=%async_computation | async-start | bytes 131072 | tf_op jit(solution)/shard_map/all_to_all | solution.py:217
  8.9 7.4 %copy-start = (f32[120,120]{1,0:T(8,128)S(1)}, f32[120,120]{1,0:T(8,128)}, u32[]{:S(2)}) copy-start(f32[120,120]{1,0:T(8,128)} %constant.82.clone) | copy-start | bytes 172804
  19.5 5.1 %copy-start.6 = (s32[8,16]{1,0:T(8,128)S(1)}, s32[8,16]{1,0:T(8,128)}, u32[]{:S(2)}) copy-start(s32[8,16]{1,0:T(8,128)} %param.13) | copy-start | bytes 1540
  20.0 9.4 %copy-start.4 = (f32[120,120]{1,0:T(8,128)S(1)}, f32[120,120]{1,0:T(8,128)}, u32[]{:S(2)}) copy-start(f32[120,120]{1,0:T(8,128)} %param.14) | copy-start | bytes 172804
  20.0 9.4 %copy-start.5 = (f32[120,120]{1,0:T(8,128)S(1)}, f32[120,120]{1,0:T(8,128)}, u32[]{:S(2)}) copy-start(f32[120,120]{1,0:T(8,128)} %constant.84.clone) | copy-start | bytes 172804
  20.0 9.4 %collective-permute-start.2 = (f32[120,128,1]{1,0,2:T(8,128)S(1)}, f32[120,128,1]{1,0,2:T(8,128)S(1)}, u32[]{:S(2)}, u32[]{:S(2)}) collective-permute-start(f32[120,128,1]{1,0,2:T(8,128)S(1)} %multiply_bitcast_fusion.1), channel_id=1, source_target_pairs={{0,2},{2,4},{4,6},{6,8},{8,10},{10,12},{12,14},{14,16},{16,18},{18... | collective-permute-start | bytes 184328 | tf_op jit(solution)/shard_map/ppermute | solution.py:18
  20.1 12.7 %collective-permute-start = (f32[120,128,1]{1,0,2:T(8,128)S(1)}, f32[120,128,1]{1,0,2:T(8,128)S(1)}, u32[]{:S(2)}, u32[]{:S(2)}) collective-permute-start(f32[120,128,1]{1,0,2:T(8,128)S(1)} %multiply_bitcast_fusion.1), channel_id=1, source_target_pairs={{0,30},{2,0},{4,2},{6,4},{8,6},{10,8},{12,10},{14,12},{16,14},{18,... | collective-permute-start | bytes 184328 | tf_op jit(solution)/shard_map/ppermute | solution.py:18
  25.2 9.8 %all-to-all-start.1 = ((s32[8,16,1]{0,2,1:T(1,128)}), s32[8,16,1]{0,2,1:T(1,128)S(1)}, u32[]{:S(2)}, u32[]{:S(2)}) async-start(s32[8,16,1]{0,2,1:T(1,128)} %copy.20), calls=%async_computation.1 | async-start | bytes 16384 | tf_op jit(solution)/shard_map/all_to_all | solution.py:218
  28.7 0.7 copy-start.9
  28.7 0.7 copy-start.10
  29.4 9.6 %copy-start.2 = (f32[120,120]{1,0:T(8,128)S(1)}, f32[120,120]{1,0:T(8,128)}, u32[]{:S(2)}) copy-start(f32[120,120]{1,0:T(8,128)} %constant.83.clone) | copy-start | bytes 172804
  29.4 5.7 %collective-permute-start.3 = (f32[120,128,1]{1,0,2:T(8,128)S(1)}, f32[120,128,1]{1,0,2:T(8,128)S(1)}, u32[]{:S(2)}, u32[]{:S(2)}) collective-permute-start(f32[120,128,1]{1,0,2:T(8,128)S(1)} %collective-permute-done.2), channel_id=1, source_target_pairs={{0,1},{2,3},{4,5},{6,7},{8,9},{10,11},{12,13},{14,15},{16,17},{18,... | collective-permute-start | bytes 184328 | tf_op jit(solution)/shard_map/ppermute | solution.py:24
  32.8 6.1 %collective-permute-start.1 = (f32[120,128,1]{1,0,2:T(8,128)S(1)}, f32[120,128,1]{1,0,2:T(8,128)S(1)}, u32[]{:S(2)}, u32[]{:S(2)}) collective-permute-start(f32[120,128,1]{1,0,2:T(8,128)S(1)} %collective-permute-done), channel_id=1, source_target_pairs={{1,0},{3,2},{5,4},{7,6},{9,8},{11,10},{13,12},{15,14},{17,16},{19,... | collective-permute-start | bytes 184328 | tf_op jit(solution)/shard_map/ppermute | solution.py:24
  35.0 3.9 %copy-start.8 = (f32[120]{0:T(128)S(1)}, f32[120]{0:T(128)}, u32[]{:S(2)}) copy-start(f32[120]{0:T(128)} %constant.93) | copy-start | bytes 1444
  35.1 4.1 %copy-start.1 = (f32[120,120]{1,0:T(8,128)S(1)}, f32[120,120]{1,0:T(8,128)}, u32[]{:S(2)}) copy-start(f32[120,120]{1,0:T(8,128)} %constant.85.clone) | copy-start | bytes 172804
  35.2 4.1 %copy-start.7 = (f32[120]{0:T(128)S(1)}, f32[120]{0:T(128)}, u32[]{:S(2)}) copy-start(f32[120]{0:T(128)} %constant.87.clone) | copy-start | bytes 1444
  39.3 0.8 %copy-start.3 = (f32[120,120]{1,0:T(8,128)S(1)}, f32[120,120]{1,0:T(8,128)}, u32[]{:S(2)}) copy-start(f32[120,120]{1,0:T(8,128)} %constant.86.clone) | copy-start | bytes 172804
  44.8 6.5 %collective-permute-start.6 = (f32[120,128,1]{1,0,2:T(8,128)S(1)}, f32[120,128,1]{1,0,2:T(8,128)S(1)}, u32[]{:S(2)}, u32[]{:S(2)}) collective-permute-start(f32[120,128,1]{1,0,2:T(8,128)S(1)} %multiply_bitcast_fusion), channel_id=1, source_target_pairs={{0,2},{2,4},{4,6},{6,8},{8,10},{10,12},{12,14},{14,16},{16,18},{18... | collective-permute-start | bytes 184328 | tf_op jit(solution)/shard_map/ppermute | solution.py:18
  44.8 8.0 %collective-permute-start.4 = (f32[120,128,1]{1,0,2:T(8,128)S(1)}, f32[120,128,1]{1,0,2:T(8,128)S(1)}, u32[]{:S(2)}, u32[]{:S(2)}) collective-permute-start(f32[120,128,1]{1,0,2:T(8,128)S(1)} %multiply_bitcast_fusion), channel_id=1, source_target_pairs={{0,30},{2,0},{4,2},{6,4},{8,6},{10,8},{12,10},{14,12},{16,14},{18,... | collective-permute-start | bytes 184328 | tf_op jit(solution)/shard_map/ppermute | solution.py:18
  51.2 3.4 %collective-permute-start.7 = (f32[120,128,1]{1,0,2:T(8,128)S(1)}, f32[120,128,1]{1,0,2:T(8,128)S(1)}, u32[]{:S(2)}, u32[]{:S(2)}) collective-permute-start(f32[120,128,1]{1,0,2:T(8,128)S(1)} %collective-permute-done.6), channel_id=1, source_target_pairs={{0,1},{2,3},{4,5},{6,7},{8,9},{10,11},{12,13},{14,15},{16,17},{18,... | collective-permute-start | bytes 184328 | tf_op jit(solution)/shard_map/ppermute | solution.py:24
  52.8 6.1 %collective-permute-start.5 = (f32[120,128,1]{1,0,2:T(8,128)S(1)}, f32[120,128,1]{1,0,2:T(8,128)S(1)}, u32[]{:S(2)}, u32[]{:S(2)}) collective-permute-start(f32[120,128,1]{1,0,2:T(8,128)S(1)} %collective-permute-done.4), channel_id=1, source_target_pairs={{1,0},{3,2},{5,4},{7,6},{9,8},{11,10},{13,12},{15,14},{17,16},{19,... | collective-permute-start | bytes 184328 | tf_op jit(solution)/shard_map/ppermute | solution.py:24
where the time goes:
time: 71.4 us; the launch traced here: 70.9 us
  starting transfers between devices  27.4 us (38%)
  waiting for transfers between devices  18.3 us (26%)
  matrix products  10.2 us (14%)
  blocking collectives  10.2 us (14%)
  local copies, waits for them, and re-layouts  4.25 us (6%)
    all_to_all x1, blocking collectives, local(): lax.all_to_all(line_field, 'wa', split_axis=1, concat_axis=2, tiled=True)  10.2 us
    ppermute x4, starting transfers between devices, shifted(): lax.ppermute(value, axis, [(i, (i + by) % count) for i in range(count)])  8.97 us
    ppermute x4, waiting for transfers between devices, from_behind(): return lax.ppermute(value, axis, pairs)  8.6 us
    ppermute x4, starting transfers between devices, from_behind(): return lax.ppermute(value, axis, pairs)  7.55 us
    all_to_all x1, starting transfers between devices, local(): lax.all_to_all(input_moments, 'wa', split_axis=2, concat_axis=1, tiled=True)  7.41 us
    all_to_all x1, waiting for transfers between devices, local(): lax.all_to_all(input_moments, 'wa', split_axis=2, concat_axis=1, tiled=True)  6.87 us
    all_to_all x1, starting transfers between devices, local(): lax.all_to_all(solid_cell_mask, 'wa', split_axis=1, concat_axis=0, tiled=...  3.47 us
    unnamed x23, local copies, waits for them, and re-layouts  2.77 us
  transfers between devices with their start and end apart: 10, of which 6 were waited for; matrix products, arithmetic and copies ran while one was open for 1% of the time, Pallas kernels for 0%

commit v1 on v0

--- a/solution.py
+++ b/solution.py
@@ -214,7 +214,12 @@
     length = input_moments.shape[1] * lax.axis_size("wa")
     cosine_table, sine_table = fourier_tables(length)
     wave_scale = wave_numbers(length)
-    line_field = lax.all_to_all(input_moments, "wa", split_axis=2, concat_axis=1, tiled=True)
+    line_field = jnp.concatenate(
+        lax.all_to_all(
+            jnp.stack(jnp.split(input_moments, lax.axis_size("wa"), axis=2)), "wa", 0, 0
+        ),
+        axis=1,
+    )
     mask_float = lax.all_to_all(
         solid_cell_mask, "wa", split_axis=1, concat_axis=0, tiled=True
     ).astype(jnp.float32)

time: 71.4 us -> 80.7 us (1.13)
  local copies, waits for them, and re-layouts: 4.25 us -> 13.5 us
    unnamed x23 -> x37, local copies, waits for them, and re-layouts: 2.77 us -> 10.2 us
    split x0 -> x1, local copies, waits for them, and re-layouts: none -> 1.29 us  [local(): jnp.split(input_moments, lax.axis_size('wa'), axis=2)]
where the time goes in v1:
time: 80.7 us; the launch traced here: 80.2 us
  starting transfers between devices  27.4 us (34%)
  waiting for transfers between devices  18.3 us (23%)
  local copies, waits for them, and re-layouts  13.5 us (17%)
  matrix products  10.2 us (13%)
  blocking collectives  10.2 us (13%)
    unnamed x37, local copies, waits for them, and re-layouts  10.2 us
    all_to_all x1, blocking collectives, local(): lax.all_to_all(line_field, 'wa', split_axis=1, concat_axis=2, tiled=True)  10.2 us
    ppermute x4, starting transfers between devices, shifted(): lax.ppermute(value, axis, [(i, (i + by) % count) for i in range(count)])  8.97 us
    ppermute x4, waiting for transfers between devices, from_behind(): return lax.ppermute(value, axis, pairs)  8.59 us
    ppermute x4, starting transfers between devices, from_behind(): return lax.ppermute(value, axis, pairs)  7.55 us
    all_to_all x1, starting transfers between devices, local(): lax.all_to_all(jnp.stack(jnp.split(input_moments, lax.axis_size('wa'), ax...  7.41 us
    all_to_all x1, waiting for transfers between devices, local(): lax.all_to_all(jnp.stack(jnp.split(input_moments, lax.axis_size('wa'), ax...  6.87 us
    all_to_all x1, starting transfers between devices, local(): lax.all_to_all(solid_cell_mask, 'wa', split_axis=1, concat_axis=0, tiled=...  3.47 us
  transfers between devices with their start and end apart: 10, of which 6 were waited for; matrix products, arithmetic and copies ran while one was open for 1% of the time, Pallas kernels for 0%

profile of v1, /device:TPU:0, one launch (start us, length us, event | category | flops | bytes accessed | tf_op | source)
XLA Modules:
  0.0 80.2 jit_solution(3723301391047521068)
XLA Ops:
  0.0 1.3 %fusion.137 = (f32[120,8,1]{0,2,1:T(1,128)S(1)}, f32[120,8,1]{0,2,1:T(1,128)S(1)}, f32[120,8,1]{0,2,1:T(1,128)S(1)}, f32[120,8,1]{0,2,1:T(1,128)S(1)}, f32[120,8...) fusion(f32[120,8,16]{0,2,1:T(8,128)} %param.12), kind=kLoop, calls=%fused_computation.195 | loop fusion | bytes 122880 | tf_op jit(solution)/shard_map/split | solution.py:219
  1.3 0.6 constant_dynamic-update-slice_fusion.15
  1.9 0.6 constant_dynamic-update-slice_fusion.14
  2.5 0.6 constant_dynamic-update-slice_fusion.13
  3.1 0.6 constant_dynamic-update-slice_fusion.12
  3.7 0.6 constant_dynamic-update-slice_fusion.11
  4.3 0.6 constant_dynamic-update-slice_fusion.10
  4.9 0.6 constant_dynamic-update-slice_fusion.9
  6.0 0.6 constant_dynamic-update-slice_fusion.7
  6.6 0.6 constant_dynamic-update-slice_fusion.6
  7.2 0.6 constant_dynamic-update-slice_fusion.5
  7.8 0.6 constant_dynamic-update-slice_fusion.4
  9.0 0.6 constant_dynamic-update-slice_fusion.2
  9.6 0.6 constant_dynamic-update-slice_fusion.1
  10.2 0.6 constant_dynamic-update-slice_fusion
  10.8 7.4 %all-to-all-start = ((f32[16,120,8,1]{1,2,3,0:T(8,128)}), f32[16,120,8,1]{1,2,3,0:T(8,128)S(1)}, u32[]{:S(2)}, u32[]{:S(2)}) async-start(f32[16,120,8,1]{1,2,3,0:T(8,128)} %constant_dynamic-update-slice_fusion), calls=%async_computation | async-start | bytes 131072 | tf_op jit(solution)/shard_map/all_to_all | solution.py:218
  18.2 6.9 %all-to-all-done = f32[16,120,8,1]{1,2,3,0:T(8,128)S(1)} async-done(((f32[16,120,8,1]{1,2,3,0:T(8,128)}), f32[16,120,8,1]{1,2,3,0:T(8,128)S(1)}, u32[]{:S(2)}, u32[]{:S(2)}) %all-to-all-start) | async-done | bytes 61472 | tf_op jit(solution)/shard_map/all_to_all | solution.py:218
  29.4 4.4 %collective-permute-start = (f32[120,128,1]{1,0,2:T(8,128)S(1)}, f32[120,128,1]{1,0,2:T(8,128)S(1)}, u32[]{:S(2)}, u32[]{:S(2)}) collective-permute-start(f32[120,128,1]{1,0,2:T(8,128)S(1)} %multiply_bitcast_fusion.1), channel_id=1, source_target_pairs={{0,30},{2,0},{4,2},{6,4},{8,6},{10,8},{12,10},{14,12},{16,14},{18,... | collective-permute-start | bytes 184328 | tf_op jit(solution)/shard_map/ppermute | solution.py:18
  33.8 0.7 copy.63
  34.5 3.5 %all-to-all-start.1 = ((s32[8,16,1]{0,2,1:T(1,128)}), s32[8,16,1]{0,2,1:T(1,128)S(1)}, u32[]{:S(2)}, u32[]{:S(2)}) async-start(s32[8,16,1]{0,2,1:T(1,128)} %copy.63), calls=%async_computation.1 | async-start | bytes 16384 | tf_op jit(solution)/shard_map/all_to_all | solution.py:223
  38.0 0.6 copy-done.9
  38.7 3.4 %collective-permute-start.3 = (f32[120,128,1]{1,0,2:T(8,128)S(1)}, f32[120,128,1]{1,0,2:T(8,128)S(1)}, u32[]{:S(2)}, u32[]{:S(2)}) collective-permute-start(f32[120,128,1]{1,0,2:T(8,128)S(1)} %collective-permute-done.2), channel_id=1, source_target_pairs={{0,1},{2,3},{4,5},{6,7},{8,9},{10,11},{12,13},{14,15},{16,17},{18,... | collective-permute-start | bytes 184328 | tf_op jit(solution)/shard_map/ppermute | solution.py:24
  42.1 1.3 %collective-permute-start.1 = (f32[120,128,1]{1,0,2:T(8,128)S(1)}, f32[120,128,1]{1,0,2:T(8,128)S(1)}, u32[]{:S(2)}, u32[]{:S(2)}) collective-permute-start(f32[120,128,1]{1,0,2:T(8,128)S(1)} %collective-permute-done), channel_id=1, source_target_pairs={{1,0},{3,2},{5,4},{7,6},{9,8},{11,10},{13,12},{15,14},{17,16},{19,... | collective-permute-start | bytes 184328 | tf_op jit(solution)/shard_map/ppermute | solution.py:24
  43.4 0.9 %all-to-all-done.1 = s32[8,16,1]{0,2,1:T(1,128)S(1)} async-done(((s32[8,16,1]{0,2,1:T(1,128)}), s32[8,16,1]{0,2,1:T(1,128)S(1)}, u32[]{:S(2)}, u32[]{:S(2)}) %all-to-all-start.1) | async-done | bytes 544 | tf_op jit(solution)/shard_map/all_to_all | solution.py:223
  44.5 3.8 %collective-permute-done.1 = f32[120,128,1]{1,0,2:T(8,128)S(1)} collective-permute-done((f32[120,128,1]{1,0,2:T(8,128)S(1)}, f32[120,128,1]{1,0,2:T(8,128)S(1)}, u32[]{:S(2)}, u32[]{:S(2)}) %collective-permute-start.1) | collective-permute-done | bytes 61472 | tf_op jit(solution)/shard_map/ppermute | solution.py:24
  54.2 4.4 %collective-permute-start.4 = (f32[120,128,1]{1,0,2:T(8,128)S(1)}, f32[120,128,1]{1,0,2:T(8,128)S(1)}, u32[]{:S(2)}, u32[]{:S(2)}) collective-permute-start(f32[120,128,1]{1,0,2:T(8,128)S(1)} %multiply_bitcast_fusion), channel_id=1, source_target_pairs={{0,30},{2,0},{4,2},{6,4},{8,6},{10,8},{12,10},{14,12},{16,14},{18,... | collective-permute-start | bytes 184328 | tf_op jit(solution)/shard_map/ppermute | solution.py:18
  58.6 2.0 %collective-permute-done.6 = f32[120,128,1]{1,0,2:T(8,128)S(1)} collective-permute-done((f32[120,128,1]{1,0,2:T(8,128)S(1)}, f32[120,128,1]{1,0,2:T(8,128)S(1)}, u32[]{:S(2)}, u32[]{:S(2)}) %collective-permute-start.6) | collective-permute-done | bytes 61472 | tf_op jit(solution)/shard_map/ppermute | solution.py:18
  60.5 1.6 %collective-permute-start.7 = (f32[120,128,1]{1,0,2:T(8,128)S(1)}, f32[120,128,1]{1,0,2:T(8,128)S(1)}, u32[]{:S(2)}, u32[]{:S(2)}) collective-permute-start(f32[120,128,1]{1,0,2:T(8,128)S(1)} %collective-permute-done.6), channel_id=1, source_target_pairs={{0,1},{2,3},{4,5},{6,7},{8,9},{10,11},{12,13},{14,15},{16,17},{18,... | collective-permute-start | bytes 184328 | tf_op jit(solution)/shard_map/ppermute | solution.py:24
  62.1 1.3 %collective-permute-start.5 = (f32[120,128,1]{1,0,2:T(8,128)S(1)}, f32[120,128,1]{1,0,2:T(8,128)S(1)}, u32[]{:S(2)}, u32[]{:S(2)}) collective-permute-start(f32[120,128,1]{1,0,2:T(8,128)S(1)} %collective-permute-done.4), channel_id=1, source_target_pairs={{1,0},{3,2},{5,4},{7,6},{9,8},{11,10},{13,12},{15,14},{17,16},{19,... | collective-permute-start | bytes 184328 | tf_op jit(solution)/shard_map/ppermute | solution.py:24
  64.0 4.3 %collective-permute-done.5 = f32[120,128,1]{1,0,2:T(8,128)S(1)} collective-permute-done((f32[120,128,1]{1,0,2:T(8,128)S(1)}, f32[120,128,1]{1,0,2:T(8,128)S(1)}, u32[]{:S(2)}, u32[]{:S(2)}) %collective-permute-start.5) | collective-permute-done | bytes 61472 | tf_op jit(solution)/shard_map/ppermute | solution.py:24
  69.4 10.2 %all_to_all.36 = f32[120,128,1]{0,2,1:T(1,128)S(1)} all-to-all(f32[120,128,1]{0,2,1:T(1,128)S(1)} %copy.64), channel_id=1, replica_groups=mesh['wa'=16,'gy'=2] {'wa'}, dimensions={1} | all-to-all | bytes 122880 | tf_op jit(solution)/shard_map/all_to_all | solution.py:249
  79.6 0.6 copy.65
  (70 shorter events, 13.0 us)
Async XLA Ops:
  10.8 14.3 %all-to-all-start = ((f32[16,120,8,1]{1,2,3,0:T(8,128)}), f32[16,120,8,1]{1,2,3,0:T(8,128)S(1)}, u32[]{:S(2)}, u32[]{:S(2)}) async-start(f32[16,120,8,1]{1,2,3,0:T(8,128)} %constant_dynamic-update-slice_fusion), calls=%async_computation | async-start | bytes 131072 | tf_op jit(solution)/shard_map/all_to_all | solution.py:218
  18.2 7.4 %copy-start = (f32[120,120]{1,0:T(8,128)S(1)}, f32[120,120]{1,0:T(8,128)}, u32[]{:S(2)}) copy-start(f32[120,120]{1,0:T(8,128)} %constant.82.clone) | copy-start | bytes 172804
  28.8 5.1 %copy-start.6 = (s32[8,16]{1,0:T(8,128)S(1)}, s32[8,16]{1,0:T(8,128)}, u32[]{:S(2)}) copy-start(s32[8,16]{1,0:T(8,128)} %param.13) | copy-start | bytes 1540
  29.3 9.4 %copy-start.4 = (f32[120,120]{1,0:T(8,128)S(1)}, f32[120,120]{1,0:T(8,128)}, u32[]{:S(2)}) copy-start(f32[120,120]{1,0:T(8,128)} %param.14) | copy-start | bytes 172804
  29.3 9.4 %copy-start.5 = (f32[120,120]{1,0:T(8,128)S(1)}, f32[120,120]{1,0:T(8,128)}, u32[]{:S(2)}) copy-start(f32[120,120]{1,0:T(8,128)} %constant.84.clone) | copy-start | bytes 172804
  29.3 9.4 %collective-permute-start.2 = (f32[120,128,1]{1,0,2:T(8,128)S(1)}, f32[120,128,1]{1,0,2:T(8,128)S(1)}, u32[]{:S(2)}, u32[]{:S(2)}) collective-permute-start(f32[120,128,1]{1,0,2:T(8,128)S(1)} %multiply_bitcast_fusion.1), channel_id=1, source_target_pairs={{0,2},{2,4},{4,6},{6,8},{8,10},{10,12},{12,14},{14,16},{16,18},{18... | collective-permute-start | bytes 184328 | tf_op jit(solution)/shard_map/ppermute | solution.py:18
  29.4 12.7 %collective-permute-start = (f32[120,128,1]{1,0,2:T(8,128)S(1)}, f32[120,128,1]{1,0,2:T(8,128)S(1)}, u32[]{:S(2)}, u32[]{:S(2)}) collective-permute-start(f32[120,128,1]{1,0,2:T(8,128)S(1)} %multiply_bitcast_fusion.1), channel_id=1, source_target_pairs={{0,30},{2,0},{4,2},{6,4},{8,6},{10,8},{12,10},{14,12},{16,14},{18,... | collective-permute-start | bytes 184328 | tf_op jit(solution)/shard_map/ppermute | solution.py:18
  34.5 9.8 %all-to-all-start.1 = ((s32[8,16,1]{0,2,1:T(1,128)}), s32[8,16,1]{0,2,1:T(1,128)S(1)}, u32[]{:S(2)}, u32[]{:S(2)}) async-start(s32[8,16,1]{0,2,1:T(1,128)} %copy.63), calls=%async_computation.1 | async-start | bytes 16384 | tf_op jit(solution)/shard_map/all_to_all | solution.py:223
  38.0 0.7 copy-start.9
  38.0 0.7 copy-start.10
  38.7 9.6 %copy-start.2 = (f32[120,120]{1,0:T(8,128)S(1)}, f32[120,120]{1,0:T(8,128)}, u32[]{:S(2)}) copy-start(f32[120,120]{1,0:T(8,128)} %constant.83.clone) | copy-start | bytes 172804
  38.7 5.7 %collective-permute-start.3 = (f32[120,128,1]{1,0,2:T(8,128)S(1)}, f32[120,128,1]{1,0,2:T(8,128)S(1)}, u32[]{:S(2)}, u32[]{:S(2)}) collective-permute-start(f32[120,128,1]{1,0,2:T(8,128)S(1)} %collective-permute-done.2), channel_id=1, source_target_pairs={{0,1},{2,3},{4,5},{6,7},{8,9},{10,11},{12,13},{14,15},{16,17},{18,... | collective-permute-start | bytes 184328 | tf_op jit(solution)/shard_map/ppermute | solution.py:24
  42.1 6.1 %collective-permute-start.1 = (f32[120,128,1]{1,0,2:T(8,128)S(1)}, f32[120,128,1]{1,0,2:T(8,128)S(1)}, u32[]{:S(2)}, u32[]{:S(2)}) collective-permute-start(f32[120,128,1]{1,0,2:T(8,128)S(1)} %collective-permute-done), channel_id=1, source_target_pairs={{1,0},{3,2},{5,4},{7,6},{9,8},{11,10},{13,12},{15,14},{17,16},{19,... | collective-permute-start | bytes 184328 | tf_op jit(solution)/shard_map/ppermute | solution.py:24
  44.3 3.9 %copy-start.8 = (f32[120]{0:T(128)S(1)}, f32[120]{0:T(128)}, u32[]{:S(2)}) copy-start(f32[120]{0:T(128)} %constant.93) | copy-start | bytes 1444
  44.4 4.1 %copy-start.1 = (f32[120,120]{1,0:T(8,128)S(1)}, f32[120,120]{1,0:T(8,128)}, u32[]{:S(2)}) copy-start(f32[120,120]{1,0:T(8,128)} %constant.85.clone) | copy-start | bytes 172804
  44.5 4.1 %copy-start.7 = (f32[120]{0:T(128)S(1)}, f32[120]{0:T(128)}, u32[]{:S(2)}) copy-start(f32[120]{0:T(128)} %constant.87.clone) | copy-start | bytes 1444
  48.6 0.8 %copy-start.3 = (f32[120,120]{1,0:T(8,128)S(1)}, f32[120,120]{1,0:T(8,128)}, u32[]{:S(2)}) copy-start(f32[120,120]{1,0:T(8,128)} %constant.86.clone) | copy-start | bytes 172804
  54.1 6.4 %collective-permute-start.6 = (f32[120,128,1]{1,0,2:T(8,128)S(1)}, f32[120,128,1]{1,0,2:T(8,128)S(1)}, u32[]{:S(2)}, u32[]{:S(2)}) collective-permute-start(f32[120,128,1]{1,0,2:T(8,128)S(1)} %multiply_bitcast_fusion), channel_id=1, source_target_pairs={{0,2},{2,4},{4,6},{6,8},{8,10},{10,12},{12,14},{14,16},{16,18},{18... | collective-permute-start | bytes 184328 | tf_op jit(solution)/shard_map/ppermute | solution.py:18
  54.2 8.0 %collective-permute-start.4 = (f32[120,128,1]{1,0,2:T(8,128)S(1)}, f32[120,128,1]{1,0,2:T(8,128)S(1)}, u32[]{:S(2)}, u32[]{:S(2)}) collective-permute-start(f32[120,128,1]{1,0,2:T(8,128)S(1)} %multiply_bitcast_fusion), channel_id=1, source_target_pairs={{0,30},{2,0},{4,2},{6,4},{8,6},{10,8},{12,10},{14,12},{16,14},{18,... | collective-permute-start | bytes 184328 | tf_op jit(solution)/shard_map/ppermute | solution.py:18
  60.5 3.4 %collective-permute-start.7 = (f32[120,128,1]{1,0,2:T(8,128)S(1)}, f32[120,128,1]{1,0,2:T(8,128)S(1)}, u32[]{:S(2)}, u32[]{:S(2)}) collective-permute-start(f32[120,128,1]{1,0,2:T(8,128)S(1)} %collective-permute-done.6), channel_id=1, source_target_pairs={{0,1},{2,3},{4,5},{6,7},{8,9},{10,11},{12,13},{14,15},{16,17},{18,... | collective-permute-start | bytes 184328 | tf_op jit(solution)/shard_map/ppermute | solution.py:24
  62.1 6.1 %collective-permute-start.5 = (f32[120,128,1]{1,0,2:T(8,128)S(1)}, f32[120,128,1]{1,0,2:T(8,128)S(1)}, u32[]{:S(2)}, u32[]{:S(2)}) collective-permute-start(f32[120,128,1]{1,0,2:T(8,128)S(1)} %collective-permute-done.4), channel_id=1, source_target_pairs={{1,0},{3,2},{5,4},{7,6},{9,8},{11,10},{13,12},{15,14},{17,16},{19,... | collective-permute-start | bytes 184328 | tf_op jit(solution)/shard_map/ppermute | solution.py:24
